TPU v7x, 32 devices: a whole 2x2x4 slice. The times are simulated.
32 devices in a mesh: tm: 8 (over y, x, core), group: 4 (over z).
Axes of the slice: x: 2, y: 2, z: 4, core: 2. Of those that a mesh axis runs over, the one named last changes fastest.
Arguments:
- tokens: bfloat16 [8, 1024, 1024], P('tm', 'group'), may hold values from -6 to 6
- conv_weight: float32 [3, 1024], replicated, may hold values from -3 to 3
- qkv_weight: bfloat16 [1024, 3072], replicated, may hold values from -0.1875 to 0.1875
- attn_out_weight: bfloat16 [1024, 1024], replicated, may hold values from -0.1875 to 0.1875
- router_weight: bfloat16 [1024, 16], replicated, may hold values from -0.375 to 0.375
- expert_ids: int32 [8, 1024, 2], P('tm', 'group'), may hold values from 0 to 15, as said below
- expert_in: bfloat16 [32, 1024, 2048], P(('tm', 'group')), may hold values from -0.1875 to 0.1875
- expert_out: bfloat16 [32, 2048, 1024], P(('tm', 'group')), may hold values from -0.09375 to 0.09375
Outputs:
- layer_out: bfloat16 [8, 1024, 1024], P('tm', 'group')
Inputs may be any that keep to these rules, and one draw needn't show every extreme that they name: `expert_ids`: each row names two different experts. In the rows of one device (one frame, 256 consecutive spatial positions) * 4 experts are named exactly 64 times each and the others share the remaining routes as evenly as possible; one expert is among the fully named ones on every device.
All inputs are finite; a program needn't handle non-finite values.
Results may differ from a plain program's by a relative error of at most 0.0095.
Values may be sent and summed in bfloat16 or wider, within the bound.
No kernel may reach another device: no remote copies, remote signals or barrier semaphores. Data moves between devices by JAX's collectives and lax.ppermute only.
A program may use at most 128 MiB of HBM per device.

v0:
```python
import math
import jax
import jax.numpy as jnp
from jax import lax
from jax.sharding import PartitionSpec as P

HD = 64


def layer_normed(values):
    values = values.astype(jnp.float32)
    centre = jnp.mean(values, -1, keepdims=True)
    spread = jnp.mean((values - centre) ** 2, -1, keepdims=True)
    return ((values - centre) / jnp.sqrt(spread + 1e-05)).astype(jnp.bfloat16)


def unit_scaled(values):
    return (values / jnp.sqrt(jnp.mean(values * values, -1, keepdims=True) + 1e-06)).astype(
        jnp.bfloat16
    )


def convolved(frames, conv_weight):
    wide = frames.astype(jnp.float32)
    padded = jnp.pad(wide, ((1, 1), (0, 0), (0, 0)))
    summed = conv_weight[0] * padded[:-2] + conv_weight[1] * wide + conv_weight[2] * padded[2:]
    return (wide + summed).astype(jnp.bfloat16)


def time_mixing(normed, qkv_weight, attn_out_weight):
    frames, across, channels = normed.shape
    heads = channels // HD
    projected = jnp.dot(
        normed.reshape(frames * across, channels), qkv_weight, preferred_element_type=jnp.float32
    )
    projected = projected.reshape(frames, across, 3, heads, HD)
    queries = unit_scaled(projected[:, :, 0])
    keys_all = unit_scaled(projected[:, :, 1])
    values_all = projected[:, :, 2].astype(jnp.bfloat16)
    scores = jnp.einsum(
        "fshd,gshd->shfg", queries, keys_all, preferred_element_type=jnp.float32
    ) / math.sqrt(HD)
    weights = jnp.exp(scores)
    weights = (weights / jnp.sum(weights, -1, keepdims=True)).astype(jnp.bfloat16)
    context = jnp.einsum(
        "shfg,gshd->fshd", weights, values_all, preferred_element_type=jnp.float32
    ).astype(jnp.bfloat16)
    mixed_out = jnp.dot(
        context.reshape(frames * across, channels),
        attn_out_weight,
        preferred_element_type=jnp.float32,
    )
    return mixed_out.astype(jnp.bfloat16).reshape(frames, across, channels)


def body(
    tokens,
    conv_weight,
    qkv_weight,
    attn_out_weight,
    router_weight,
    expert_ids,
    expert_in,
    expert_out,
):
    shards = lax.axis_size("tm")
    groups = lax.axis_size("group")
    classes = groups // 2
    mine = lax.axis_index("group") // 2
    spatial, channels = tokens.shape[1:]
    across = spatial // shards
    experts = router_weight.shape[1]
    capacity = 4 * spatial // experts

    def swapped(rows, step):
        if step == 0:
            return rows
        return lax.ppermute(rows, "group", [(i, i ^ step) for i in range(groups)])

    routed = expert_ids.reshape(spatial, 2)
    ids = [swapped(routed, step) for step in range(groups)]
    received = lax.all_to_all(
        tokens.reshape(1, shards, across, channels), "tm", split_axis=1, concat_axis=0, tiled=True
    ).reshape(shards, across, channels)
    stream_one = convolved(received, conv_weight)
    attended = time_mixing(layer_normed(stream_one), qkv_weight, attn_out_weight)
    stream_two = (stream_one.astype(jnp.float32) + attended.astype(jnp.float32)).astype(
        jnp.bfloat16
    )
    stream = lax.all_to_all(
        stream_two.reshape(shards, 1, across, channels),
        "tm",
        split_axis=0,
        concat_axis=1,
        tiled=True,
    ).reshape(spatial, channels)
    home = jnp.arange(shards, dtype=jnp.int32) * classes + mine
    blocks = [swapped(stream, step) for step in range(groups)]
    partials = []
    for step in range(groups):
        rows = layer_normed(blocks[step])
        logits = jnp.dot(rows, router_weight, preferred_element_type=jnp.float32)
        matches = ids[step][:, :, None] == jnp.arange(experts, dtype=jnp.int32)
        chosen = jnp.sum(jnp.where(matches, logits[:, None, :], 0.0), -1)
        gates = jax.nn.sigmoid(chosen)
        shares = gates / jnp.sum(gates, -1, keepdims=True)
        here = ids[step][:, :, None] == home
        weight = jnp.sum(jnp.where(here, shares[:, :, None], 0.0), 1)
        member = jnp.any(here, 1)
        order = jnp.arange(spatial, dtype=jnp.int32)
        earlier = (order[:, None] > order[None, :]).astype(jnp.bfloat16)
        rank = jnp.dot(
            earlier, member.astype(jnp.bfloat16), preferred_element_type=jnp.float32
        ).astype(jnp.int32)
        slots = jnp.arange(capacity, dtype=jnp.int32)
        picks = member[:, :, None] & (rank[:, :, None] == slots)
        send = picks.astype(jnp.bfloat16).reshape(spatial, shards * capacity)
        back = jnp.where(picks, weight[:, :, None], 0.0).astype(jnp.bfloat16)
        back = back.reshape(spatial, shards * capacity)
        outbox = lax.dot_general(
            send, rows, (((0,), (0,)), ((), ())), preferred_element_type=jnp.float32
        ).astype(jnp.bfloat16)
        inbox = lax.all_to_all(
            outbox.reshape(shards, capacity, channels),
            "tm",
            split_axis=0,
            concat_axis=0,
            tiled=True,
        ).reshape(shards * capacity, channels)
        hidden = jax.nn.gelu(
            jnp.dot(inbox, expert_in[0], preferred_element_type=jnp.float32)
        ).astype(jnp.bfloat16)
        partial = jnp.dot(hidden, expert_out[0], preferred_element_type=jnp.float32)
        returned = lax.all_to_all(
            partial.astype(jnp.bfloat16).reshape(shards, capacity, channels),
            "tm",
            split_axis=0,
            concat_axis=0,
            tiled=True,
        ).reshape(shards * capacity, channels)
        mixed = jnp.dot(back, returned, preferred_element_type=jnp.float32)
        if step:
            mixed = swapped(mixed.astype(jnp.bfloat16), step).astype(jnp.float32)
        partials.append(mixed)
    total = stream.astype(jnp.float32)
    for mixed in partials:
        total = total + mixed
    return total.astype(jnp.bfloat16).reshape(1, spatial, channels)


def solution(mesh):
    placed = (
        P("tm", "group", None),
        P(),
        P(),
        P(),
        P(),
        P("tm", "group", None),
        P(("tm", "group"), None, None),
        P(("tm", "group"), None, None),
    )
    return jax.shard_map(
        body, mesh=mesh, in_specs=placed, out_specs=P("tm", "group", None), check_vma=False
    )
```

profile of v0, /device:TPU:10, one launch (start us, length us, event | category | flops | bytes accessed | tf_op | source)
XLA Modules:
  0.0 279.0 jit_solution(12095422469277350351)
XLA Ops:
  0.5 2.6 collective-permute-start.3
  3.5 4.3 %all-to-all-start = ((bf16[1,8,32,1024]{3,2,0,1:T(8,128)(2,1)}), bf16[1,8,32,1024]{3,2,0,1:T(8,128)(2,1)S(1)}, u32[]{:S(2)}, u32[]{:S(2)}) async-start(bf16[1,8,32,1024]{3,2,0,1:T(8,128)(2,1)} %bitcast.183), calls=%async_computation | async-start | bytes 1048576 | tf_op jit(solution)/shard_map/all_to_all | solution.py:82
  8.6 8.7 %copy.63 = bf16[1024,3072]{0,1:T(8,128)(2,1)} copy(bf16[1024,3072]{1,0:T(8,128)(2,1)} %param.10) | data formatting | bytes 12582912 | tf_op args[2]
  20.5 5.7 %fusion.119 = f32[8,32,3,16,64]{4,1,3,2,0:T(8,128)S(1)} fusion(bf16[3,16,64,1024,1]{3,2,1,0,4:T(8,128)(2,1)} %bitcast.172, bf16[8,32,1024]{2,1,0:T(8,128)(2,1)S(1)} %get-tuple-element.16, f32[8,32]{1,0:T(8,128)S(1)} %add_sqrt_fusion.3, f32[8,32]{1,0:T(8,128)S(1)} %broadcast_multiply_fusion.1), kind=kOutput, calls=%fused_computation.138 | convolution fusion | flops 1611661312 | bytes 9963520 | tf_op jit(solution)/shard_map/dot_general | solution.py:33
  27.7 1.4 divide_convert_fusion.2
  29.1 2.8 %fusion.56 = (f32[32,16,8]{2,1,0:T(8,128)S(1)}, f32[32,16,8,8]{2,3,1,0:T(8,128)S(1)}) fusion(bf16[8,32,16,64]{3,1,2,0:T(8,128)(2,1)S(1)} %get-tuple-element.18, bf16[8,32,16,64]{3,1,2,0:T(8,128)(2,1)S(1)} %get-tuple-element.17), kind=kOutput, calls=%fused_computation.61 | convolution fusion | flops 4255744 | bytes 1196032 | tf_op jit(solution)/shard_map/fshd,gshd->shfg/dot_general | solution.py:40
  32.0 1.5 fusion.69
  34.6 1.9 reshape.364
  38.3 4.2 %all-to-all-start.1 = ((bf16[8,1,32,1024]{3,2,1,0:T(8,128)(2,1)}), bf16[8,1,32,1024]{3,2,1,0:T(8,128)(2,1)S(1)}, u32[]{:S(2)}, u32[]{:S(2)}) async-start(bf16[8,1,32,1024]{3,2,1,0:T(8,128)(2,1)} %fusion.117), calls=%async_computation.1 | async-start | bytes 1048576 | tf_op jit(solution)/shard_map/all_to_all | solution.py:90
  45.3 5.5 %all-to-all-done.1 = bf16[8,1,32,1024]{3,2,1,0:T(8,128)(2,1)S(1)} async-done(((bf16[8,1,32,1024]{3,2,1,0:T(8,128)(2,1)}), bf16[8,1,32,1024]{3,2,1,0:T(8,128)(2,1)S(1)}, u32[]{:S(2)}, u32[]{:S(2)}) %all-to-all-start.1) | async-done | bytes 524320 | tf_op jit(solution)/shard_map/all_to_all | solution.py:90
  50.8 1.3 collective-permute-start.1
  52.1 2.1 collective-permute-start.4
  56.8 2.4 convolution_convert_fusion.3
  59.2 5.6 %all-to-all-start.2 = ((bf16[8,64,1024]{2,1,0:T(8,128)(2,1)}), bf16[8,64,1024]{2,1,0:T(8,128)(2,1)}, u32[]{:S(2)}, u32[]{:S(2)}) async-start(bf16[8,64,1024]{2,1,0:T(8,128)(2,1)} %bitcast.173), calls=%async_computation.2 | async-start | bytes 2097152 | tf_op jit(solution)/shard_map/all_to_all | solution.py:123
  66.6 7.6 %collective-permute-done.1 = bf16[256,1024]{1,0:T(8,128)(2,1)} collective-permute-done((bf16[256,1024]{1,0:T(8,128)(2,1)S(1)}, bf16[256,1024]{1,0:T(8,128)(2,1)}, u32[]{:S(2)}, u32[]{:S(2)}) %collective-permute-start.1) | collective-permute-done | bytes 524320 | tf_op jit(solution)/shard_map/ppermute | solution.py:78
  75.4 1.3 fusion.89
  78.2 10.9 %collective-permute-done.4 = bf16[256,1024]{1,0:T(8,128)(2,1)} collective-permute-done((bf16[256,1024]{1,0:T(8,128)(2,1)S(1)}, bf16[256,1024]{1,0:T(8,128)(2,1)}, u32[]{:S(2)}, u32[]{:S(2)}) %collective-permute-start.4) | collective-permute-done | bytes 524320 | tf_op jit(solution)/shard_map/ppermute | solution.py:78
  90.3 1.3 fusion.87
  93.1 7.3 %collective-permute-done.7 = bf16[256,1024]{1,0:T(8,128)(2,1)S(1)} collective-permute-done((bf16[256,1024]{1,0:T(8,128)(2,1)S(1)}, bf16[256,1024]{1,0:T(8,128)(2,1)S(1)}, u32[]{:S(2)}, u32[]{:S(2)}) %collective-permute-start.7) | collective-permute-done | bytes 524320 | tf_op jit(solution)/shard_map/ppermute | solution.py:78
  103.1 1.4 convolution_convert_fusion.2
  104.6 4.2 %all-to-all-start.4 = ((bf16[8,64,1024]{2,1,0:T(8,128)(2,1)}), bf16[8,64,1024]{2,1,0:T(8,128)(2,1)}, u32[]{:S(2)}, u32[]{:S(2)}) async-start(bf16[8,64,1024]{2,1,0:T(8,128)(2,1)} %bitcast.175), calls=%async_computation.4 | async-start | bytes 2097152 | tf_op jit(solution)/shard_map/all_to_all | solution.py:123
  109.5 1.3 fusion.176
  111.5 2.5 convolution_convert_fusion.1
  113.9 7.9 %all-to-all-done.4 = bf16[8,64,1024]{2,1,0:T(8,128)(2,1)} async-done(((bf16[8,64,1024]{2,1,0:T(8,128)(2,1)}), bf16[8,64,1024]{2,1,0:T(8,128)(2,1)}, u32[]{:S(2)}, u32[]{:S(2)}) %all-to-all-start.4) | async-done | bytes 1048608 | tf_op jit(solution)/shard_map/all_to_all | solution.py:123
  121.9 5.6 %all-to-all-start.6 = ((bf16[8,64,1024]{2,1,0:T(8,128)(2,1)}), bf16[8,64,1024]{2,1,0:T(8,128)(2,1)}, u32[]{:S(2)}, u32[]{:S(2)}) async-start(bf16[8,64,1024]{2,1,0:T(8,128)(2,1)} %bitcast.174), calls=%async_computation.6 | async-start | bytes 2097152 | tf_op jit(solution)/shard_map/all_to_all | solution.py:123
  129.0 1.4 convolution_convert_fusion
  130.4 11.1 %all-to-all-done.6 = bf16[8,64,1024]{2,1,0:T(8,128)(2,1)} async-done(((bf16[8,64,1024]{2,1,0:T(8,128)(2,1)}), bf16[8,64,1024]{2,1,0:T(8,128)(2,1)}, u32[]{:S(2)}, u32[]{:S(2)}) %all-to-all-start.6) | async-done | bytes 1048608 | tf_op jit(solution)/shard_map/all_to_all | solution.py:123
  141.5 5.6 %all-to-all-start.8 = ((bf16[8,64,1024]{2,1,0:T(8,128)(2,1)}), bf16[8,64,1024]{2,1,0:T(8,128)(2,1)}, u32[]{:S(2)}, u32[]{:S(2)}) async-start(bf16[8,64,1024]{2,1,0:T(8,128)(2,1)} %bitcast.176), calls=%async_computation.8 | async-start | bytes 2097152 | tf_op jit(solution)/shard_map/all_to_all | solution.py:123
  147.1 9.3 %fusion.60 = bf16[512,1024]{1,0:T(8,128)(2,1)} fusion(bf16[1,2048,1024]{2,1,0:T(8,128)(2,1)} %param.15, bf16[512,1024]{1,0:T(8,128)(2,1)} %bitcast.31, bf16[1,1024,2048]{2,1,0:T(8,128)(2,1)} %param.14), kind=kOutput, calls=%fused_computation.71 | convolution fusion | flops 4304928768 | bytes 10485760 | tf_op jit(solution)/shard_map/dot_general | solution.py:133
  156.5 4.6 %all-to-all-done.8 = bf16[8,64,1024]{2,1,0:T(8,128)(2,1)} async-done(((bf16[8,64,1024]{2,1,0:T(8,128)(2,1)}), bf16[8,64,1024]{2,1,0:T(8,128)(2,1)}, u32[]{:S(2)}, u32[]{:S(2)}) %all-to-all-start.8) | async-done | bytes 1048608 | tf_op jit(solution)/shard_map/all_to_all | solution.py:123
  161.1 5.6 %all-to-all-start.5 = ((bf16[8,64,1024]{2,1,0:T(8,128)(2,1)}), bf16[8,64,1024]{2,1,0:T(8,128)(2,1)}, u32[]{:S(2)}, u32[]{:S(2)}) async-start(bf16[8,64,1024]{2,1,0:T(8,128)(2,1)} %bitcast.180), calls=%async_computation.5 | async-start | bytes 2097152 | tf_op jit(solution)/shard_map/all_to_all | solution.py:134
  166.8 9.4 %fusion.63 = bf16[512,1024]{1,0:T(8,128)(2,1)} fusion(bf16[1,2048,1024]{2,1,0:T(8,128)(2,1)} %param.15, bf16[512,1024]{1,0:T(8,128)(2,1)} %bitcast.37, bf16[1,1024,2048]{2,1,0:T(8,128)(2,1)} %param.14), kind=kOutput, calls=%fused_computation.72 | convolution fusion | flops 4304928768 | bytes 10485760 | tf_op jit(solution)/shard_map/dot_general | solution.py:133
  176.1 4.6 %all-to-all-done.5 = bf16[8,64,1024]{2,1,0:T(8,128)(2,1)} async-done(((bf16[8,64,1024]{2,1,0:T(8,128)(2,1)}), bf16[8,64,1024]{2,1,0:T(8,128)(2,1)}, u32[]{:S(2)}, u32[]{:S(2)}) %all-to-all-start.5) | async-done | bytes 1048608 | tf_op jit(solution)/shard_map/all_to_all | solution.py:134
  180.8 5.6 %all-to-all-start.7 = ((bf16[8,64,1024]{2,1,0:T(8,128)(2,1)}), bf16[8,64,1024]{2,1,0:T(8,128)(2,1)}, u32[]{:S(2)}, u32[]{:S(2)}) async-start(bf16[8,64,1024]{2,1,0:T(8,128)(2,1)} %bitcast.181), calls=%async_computation.7 | async-start | bytes 2097152 | tf_op jit(solution)/shard_map/all_to_all | solution.py:134
  186.4 9.4 %fusion.66 = bf16[512,1024]{1,0:T(8,128)(2,1)} fusion(bf16[1,2048,1024]{2,1,0:T(8,128)(2,1)} %param.15, bf16[512,1024]{1,0:T(8,128)(2,1)} %bitcast.43, bf16[1,1024,2048]{2,1,0:T(8,128)(2,1)} %param.14), kind=kOutput, calls=%fused_computation.73 | convolution fusion | flops 4304928768 | bytes 10485760 | tf_op jit(solution)/shard_map/dot_general | solution.py:133
  195.8 4.6 %all-to-all-done.7 = bf16[8,64,1024]{2,1,0:T(8,128)(2,1)} async-done(((bf16[8,64,1024]{2,1,0:T(8,128)(2,1)}), bf16[8,64,1024]{2,1,0:T(8,128)(2,1)}, u32[]{:S(2)}, u32[]{:S(2)}) %all-to-all-start.7) | async-done | bytes 1048608 | tf_op jit(solution)/shard_map/all_to_all | solution.py:134
  200.4 5.6 %all-to-all-start.9 = ((bf16[8,64,1024]{2,1,0:T(8,128)(2,1)}), bf16[8,64,1024]{2,1,0:T(8,128)(2,1)}, u32[]{:S(2)}, u32[]{:S(2)}) async-start(bf16[8,64,1024]{2,1,0:T(8,128)(2,1)} %bitcast.179), calls=%async_computation.9 | async-start | bytes 2097152 | tf_op jit(solution)/shard_map/all_to_all | solution.py:134
  206.0 9.4 %fusion.57 = bf16[512,1024]{1,0:T(8,128)(2,1)} fusion(bf16[1,2048,1024]{2,1,0:T(8,128)(2,1)} %param.15, bf16[512,1024]{1,0:T(8,128)(2,1)} %bitcast.23, bf16[1,1024,2048]{2,1,0:T(8,128)(2,1)} %param.14), kind=kOutput, calls=%fused_computation.70 | convolution fusion | flops 4304928768 | bytes 10485760 | tf_op jit(solution)/shard_map/dot_general | solution.py:133
  215.5 2.5 fusion.70
  218.0 2.0 all-to-all-done.9
  220.0 5.8 %all-to-all-start.3 = ((bf16[8,64,1024]{2,1,0:T(8,128)(2,1)}), bf16[8,64,1024]{2,1,0:T(8,128)(2,1)}, u32[]{:S(2)}, u32[]{:S(2)}) async-start(bf16[8,64,1024]{2,1,0:T(8,128)(2,1)} %bitcast.178), calls=%async_computation.3 | async-start | bytes 2097152 | tf_op jit(solution)/shard_map/all_to_all | solution.py:134
  225.8 2.5 fusion.71
  228.3 2.5 fusion.72
  230.9 1.5 collective-permute-start.8
  232.3 7.5 %all-to-all-done.3 = bf16[8,64,1024]{2,1,0:T(8,128)(2,1)} async-done(((bf16[8,64,1024]{2,1,0:T(8,128)(2,1)}), bf16[8,64,1024]{2,1,0:T(8,128)(2,1)}, u32[]{:S(2)}, u32[]{:S(2)}) %all-to-all-start.3) | async-done | bytes 1048608 | tf_op jit(solution)/shard_map/all_to_all | solution.py:134
  239.8 23.7 %collective-permute-done.5 = bf16[256,1024]{1,0:T(8,128)(2,1)} collective-permute-done((bf16[256,1024]{1,0:T(8,128)(2,1)}, bf16[256,1024]{1,0:T(8,128)(2,1)}, u32[]{:S(2)}, u32[]{:S(2)}) %collective-permute-start.5) | collective-permute-done | bytes 524320 | tf_op jit(solution)/shard_map/ppermute | solution.py:78
  263.5 12.5 %collective-permute-done.8 = bf16[256,1024]{1,0:T(8,128)(2,1)} collective-permute-done((bf16[256,1024]{1,0:T(8,128)(2,1)}, bf16[256,1024]{1,0:T(8,128)(2,1)}, u32[]{:S(2)}, u32[]{:S(2)}) %collective-permute-start.8) | collective-permute-done | bytes 524320 | tf_op jit(solution)/shard_map/ppermute | solution.py:78
  276.0 3.0 %fusion.116 = bf16[1,256,1024]{2,1,0:T(8,128)(2,1)} fusion(bf16[256,1024]{1,0:T(8,128)(2,1)} %collective-permute-done.8, bf16[256,1024]{1,0:T(8,128)(2,1)} %collective-permute-done.5, bf16[256,1024]{1,0:T(8,128)(2,1)S(1)} %collective-permute-done.2, bf16[8,64,1024]{2,1,0:T(8,128)(2,1)} %all-to-all-done.3, bf16[256,1024]{1,0:T(8,128)(2,1)S(1)} %bitcast.171, ...), kind=kOutput, calls=%fused_computation.135 | convolution fusion | flops 271187968 | bytes 3684352 | tf_op jit(solution)/shard_map/dot_general | solution.py:141
  (119 shorter events, 27.2 us)
Async XLA Ops:
  0.0 36.6 %copy-start = (bf16[1024,1024]{1,0:T(8,128)(2,1)S(1)}, bf16[1024,1024]{1,0:T(8,128)(2,1)}, u32[]{:S(2)}) copy-start(bf16[1024,1024]{1,0:T(8,128)(2,1)} %param.11) | copy-start | bytes 6291460
  0.0 18.0 %collective-permute-start = (s32[256,2]{0,1:T(2,128)}, s32[256,2]{0,1:T(2,128)S(1)}, u32[]{:S(2)}, u32[]{:S(2)}) collective-permute-start(s32[256,2]{0,1:T(2,128)} %bitcast.185), channel_id=1, source_target_pairs={{0,1},{1,0},{2,3},{3,2},{4,5},{5,4},{6,7},{7,6},{8,9},{9,8},{10,11... | collective-permute-start | bytes 6152 | tf_op jit(solution)/shard_map/ppermute | solution.py:78
  0.5 17.5 %collective-permute-start.3 = (s32[256,2]{0,1:T(2,128)}, s32[256,2]{0,1:T(2,128)S(1)}, u32[]{:S(2)}, u32[]{:S(2)}) collective-permute-start(s32[256,2]{0,1:T(2,128)} %bitcast.186), channel_id=1, source_target_pairs={{0,2},{1,3},{2,0},{3,1},{4,6},{5,7},{6,4},{7,5},{8,10},{9,11},{10,... | collective-permute-start | bytes 6152 | tf_op jit(solution)/shard_map/ppermute | solution.py:78
  3.0 15.0 %collective-permute-start.6 = (s32[256,2]{0,1:T(2,128)}, s32[256,2]{0,1:T(2,128)S(1)}, u32[]{:S(2)}, u32[]{:S(2)}) collective-permute-start(s32[256,2]{0,1:T(2,128)} %bitcast.187), channel_id=1, source_target_pairs={{0,3},{1,2},{2,1},{3,0},{4,7},{5,6},{6,5},{7,4},{8,11},{9,10},{10,... | collective-permute-start | bytes 6152 | tf_op jit(solution)/shard_map/ppermute | solution.py:78
  3.5 16.2 %all-to-all-start = ((bf16[1,8,32,1024]{3,2,0,1:T(8,128)(2,1)}), bf16[1,8,32,1024]{3,2,0,1:T(8,128)(2,1)S(1)}, u32[]{:S(2)}, u32[]{:S(2)}) async-start(bf16[1,8,32,1024]{3,2,0,1:T(8,128)(2,1)} %bitcast.183), calls=%async_computation | async-start | bytes 1048576 | tf_op jit(solution)/shard_map/all_to_all | solution.py:82
  8.6 9.4 %copy-start.24 = (s32[8]{0:T(128)}, s32[8]{0:T(128)S(1)}, u32[]{:S(2)}) copy-start(s32[8]{0:T(128)S(1)} %multiply_add_fusion) | copy-start | bytes 100
  8.6 9.4 %copy-start.4 = (s32[1,256,2]{1,2,0:T(2,128)S(1)}, s32[1,256,2]{1,2,0:T(2,128)}, u32[]{:S(2)}) copy-start(s32[1,256,2]{1,2,0:T(2,128)} %param.13) | copy-start | bytes 6148
  18.0 8.2 %copy-start.5 = (s32[256,2]{0,1:T(2,128)}, s32[256,2]{0,1:T(2,128)S(1)}, u32[]{:S(2)}) copy-start(s32[256,2]{0,1:T(2,128)S(1)} %collective-permute-done.3) | copy-start | bytes 6148
  18.0 8.2 %copy-start.7 = (s32[256,2]{0,1:T(2,128)}, s32[256,2]{0,1:T(2,128)S(1)}, u32[]{:S(2)}) copy-start(s32[256,2]{0,1:T(2,128)S(1)} %collective-permute-done.6) | copy-start | bytes 6148
  18.1 1.7 copy-start.20
  18.1 24.4 %copy-start.22 = (pred[256,8]{0,1:T(8,128)(4,1)}, pred[256,8]{0,1:T(8,128)(4,1)S(1)}, u32[]{:S(2)}) copy-start(pred[256,8]{0,1:T(8,128)(4,1)S(1)} %get-tuple-element.12) | copy-start | bytes 6148
  18.1 24.5 %copy-start.18 = (pred[256,8]{0,1:T(8,128)(4,1)}, pred[256,8]{0,1:T(8,128)(4,1)S(1)}, u32[]{:S(2)}) copy-start(pred[256,8]{0,1:T(8,128)(4,1)S(1)} %get-tuple-element.14) | copy-start | bytes 6148
  18.1 25.8 %copy-start.10 = (pred[256,8]{0,1:T(8,128)(4,1)}, pred[256,8]{0,1:T(8,128)(4,1)S(1)}, u32[]{:S(2)}) copy-start(pred[256,8]{0,1:T(8,128)(4,1)S(1)} %get-tuple-element.11) | copy-start | bytes 6148
  38.3 12.5 %all-to-all-start.1 = ((bf16[8,1,32,1024]{3,2,1,0:T(8,128)(2,1)}), bf16[8,1,32,1024]{3,2,1,0:T(8,128)(2,1)S(1)}, u32[]{:S(2)}, u32[]{:S(2)}) async-start(bf16[8,1,32,1024]{3,2,1,0:T(8,128)(2,1)} %fusion.117), calls=%async_computation.1 | async-start | bytes 1048576 | tf_op jit(solution)/shard_map/all_to_all | solution.py:90
  42.7 1.3 copy-start.16
  43.9 0.6 copy-start.12
  50.8 23.4 %collective-permute-start.1 = (bf16[256,1024]{1,0:T(8,128)(2,1)S(1)}, bf16[256,1024]{1,0:T(8,128)(2,1)}, u32[]{:S(2)}, u32[]{:S(2)}) collective-permute-start(bf16[256,1024]{1,0:T(8,128)(2,1)S(1)} %bitcast.167), channel_id=1, source_target_pairs={{0,1},{1,0},{2,3},{3,2},{4,5},{5,4},{6,7},{7,6},{8,9},{9,8},{10,11... | collective-permute-start | bytes 1572872 | tf_op jit(solution)/shard_map/ppermute | solution.py:78
  52.1 37.0 %collective-permute-start.4 = (bf16[256,1024]{1,0:T(8,128)(2,1)S(1)}, bf16[256,1024]{1,0:T(8,128)(2,1)}, u32[]{:S(2)}, u32[]{:S(2)}) collective-permute-start(bf16[256,1024]{1,0:T(8,128)(2,1)S(1)} %bitcast.168), channel_id=1, source_target_pairs={{0,2},{1,3},{2,0},{3,1},{4,6},{5,7},{6,4},{7,5},{8,10},{9,11},{10,... | collective-permute-start | bytes 1572872 | tf_op jit(solution)/shard_map/ppermute | solution.py:78
  54.3 46.2 %collective-permute-start.7 = (bf16[256,1024]{1,0:T(8,128)(2,1)S(1)}, bf16[256,1024]{1,0:T(8,128)(2,1)S(1)}, u32[]{:S(2)}, u32[]{:S(2)}) collective-permute-start(bf16[256,1024]{1,0:T(8,128)(2,1)S(1)} %bitcast.169), channel_id=1, source_target_pairs={{0,3},{1,2},{2,1},{3,0},{4,7},{5,6},{6,5},{7,4},{8,11},{9,10},{10,... | collective-permute-start | bytes 1572872 | tf_op jit(solution)/shard_map/ppermute | solution.py:78
  59.2 45.4 %all-to-all-start.2 = ((bf16[8,64,1024]{2,1,0:T(8,128)(2,1)}), bf16[8,64,1024]{2,1,0:T(8,128)(2,1)}, u32[]{:S(2)}, u32[]{:S(2)}) async-start(bf16[8,64,1024]{2,1,0:T(8,128)(2,1)} %bitcast.173), calls=%async_computation.2 | async-start | bytes 2097152 | tf_op jit(solution)/shard_map/all_to_all | solution.py:123
  64.7 13.2 %copy-start.3 = (bf16[1024,16]{0,1:T(8,128)(2,1)S(1)}, bf16[1024,16]{0,1:T(8,128)(2,1)}, u32[]{:S(2)}) copy-start(bf16[1024,16]{0,1:T(8,128)(2,1)} %param.12) | copy-start | bytes 98308
  64.7 35.9 %copy-start.6 = (s32[256,2]{0,1:T(2,128)S(1)}, s32[256,2]{0,1:T(2,128)}, u32[]{:S(2)}) copy-start(s32[256,2]{0,1:T(2,128)} %copy-done.5) | copy-start | bytes 6148
  91.6 19.1 %copy-start.8 = (s32[256,2]{0,1:T(2,128)S(1)}, s32[256,2]{0,1:T(2,128)}, u32[]{:S(2)}) copy-start(s32[256,2]{0,1:T(2,128)} %copy-done.7) | copy-start | bytes 6148
  92.9 10.3 %copy-start.2 = (bf16[256,1024]{1,0:T(8,128)(2,1)}, bf16[256,1024]{1,0:T(8,128)(2,1)S(1)}, u32[]{:S(2)}) copy-start(bf16[256,1024]{1,0:T(8,128)(2,1)S(1)} %fusion.88) | copy-start | bytes 1572868
  100.6 2.5 copy-start.9
  103.1 25.8 %copy-start.1 = (bf16[256,1024]{1,0:T(8,128)(2,1)S(1)}, bf16[256,1024]{1,0:T(8,128)(2,1)}, u32[]{:S(2)}) copy-start(bf16[256,1024]{1,0:T(8,128)(2,1)} %fusion.86) | copy-start | bytes 1572868
  104.6 17.3 %all-to-all-start.4 = ((bf16[8,64,1024]{2,1,0:T(8,128)(2,1)}), bf16[8,64,1024]{2,1,0:T(8,128)(2,1)}, u32[]{:S(2)}, u32[]{:S(2)}) async-start(bf16[8,64,1024]{2,1,0:T(8,128)(2,1)} %bitcast.175), calls=%async_computation.4 | async-start | bytes 2097152 | tf_op jit(solution)/shard_map/all_to_all | solution.py:123
  121.9 19.6 %all-to-all-start.6 = ((bf16[8,64,1024]{2,1,0:T(8,128)(2,1)}), bf16[8,64,1024]{2,1,0:T(8,128)(2,1)}, u32[]{:S(2)}, u32[]{:S(2)}) async-start(bf16[8,64,1024]{2,1,0:T(8,128)(2,1)} %bitcast.174), calls=%async_computation.6 | async-start | bytes 2097152 | tf_op jit(solution)/shard_map/all_to_all | solution.py:123
  141.5 19.6 %all-to-all-start.8 = ((bf16[8,64,1024]{2,1,0:T(8,128)(2,1)}), bf16[8,64,1024]{2,1,0:T(8,128)(2,1)}, u32[]{:S(2)}, u32[]{:S(2)}) async-start(bf16[8,64,1024]{2,1,0:T(8,128)(2,1)} %bitcast.176), calls=%async_computation.8 | async-start | bytes 2097152 | tf_op jit(solution)/shard_map/all_to_all | solution.py:123
  161.1 19.6 %all-to-all-start.5 = ((bf16[8,64,1024]{2,1,0:T(8,128)(2,1)}), bf16[8,64,1024]{2,1,0:T(8,128)(2,1)}, u32[]{:S(2)}, u32[]{:S(2)}) async-start(bf16[8,64,1024]{2,1,0:T(8,128)(2,1)} %bitcast.180), calls=%async_computation.5 | async-start | bytes 2097152 | tf_op jit(solution)/shard_map/all_to_all | solution.py:134
  180.8 19.6 %all-to-all-start.7 = ((bf16[8,64,1024]{2,1,0:T(8,128)(2,1)}), bf16[8,64,1024]{2,1,0:T(8,128)(2,1)}, u32[]{:S(2)}, u32[]{:S(2)}) async-start(bf16[8,64,1024]{2,1,0:T(8,128)(2,1)} %bitcast.181), calls=%async_computation.7 | async-start | bytes 2097152 | tf_op jit(solution)/shard_map/all_to_all | solution.py:134
  200.4 19.6 %all-to-all-start.9 = ((bf16[8,64,1024]{2,1,0:T(8,128)(2,1)}), bf16[8,64,1024]{2,1,0:T(8,128)(2,1)}, u32[]{:S(2)}, u32[]{:S(2)}) async-start(bf16[8,64,1024]{2,1,0:T(8,128)(2,1)} %bitcast.179), calls=%async_computation.9 | async-start | bytes 2097152 | tf_op jit(solution)/shard_map/all_to_all | solution.py:134
  206.0 9.4 %copy-start.17 = (s32[256,8]{0,1:T(8,128)S(1)}, s32[256,8]{0,1:T(8,128)}, u32[]{:S(2)}) copy-start(s32[256,8]{0,1:T(8,128)} %copy-done.16) | copy-start | bytes 24580
  206.0 9.4 %copy-start.23 = (pred[256,8]{0,1:T(8,128)(4,1)S(1)}, pred[256,8]{0,1:T(8,128)(4,1)}, u32[]{:S(2)}) copy-start(pred[256,8]{0,1:T(8,128)(4,1)} %copy-done.22) | copy-start | bytes 6148
  215.4 10.4 %copy-start.15 = (s32[256,8]{0,1:T(8,128)S(1)}, s32[256,8]{0,1:T(8,128)}, u32[]{:S(2)}) copy-start(s32[256,8]{0,1:T(8,128)} %convolution_convert_fusion.7) | copy-start | bytes 24580
  215.4 10.4 %copy-start.21 = (pred[256,8]{0,1:T(8,128)(4,1)S(1)}, pred[256,8]{0,1:T(8,128)(4,1)}, u32[]{:S(2)}) copy-start(pred[256,8]{0,1:T(8,128)(4,1)} %copy-done.20) | copy-start | bytes 6148
  215.4 12.9 %copy-start.14 = (s32[256,8]{0,1:T(8,128)S(1)}, s32[256,8]{0,1:T(8,128)}, u32[]{:S(2)}) copy-start(s32[256,8]{0,1:T(8,128)} %convolution_convert_fusion.6) | copy-start | bytes 24580
  215.4 12.9 %copy-start.19 = (pred[256,8]{0,1:T(8,128)(4,1)S(1)}, pred[256,8]{0,1:T(8,128)(4,1)}, u32[]{:S(2)}) copy-start(pred[256,8]{0,1:T(8,128)(4,1)} %copy-done.18) | copy-start | bytes 6148
  218.0 21.8 %collective-permute-start.2 = (bf16[256,1024]{1,0:T(8,128)(2,1)}, bf16[256,1024]{1,0:T(8,128)(2,1)S(1)}, u32[]{:S(2)}, u32[]{:S(2)}) collective-permute-start(bf16[256,1024]{1,0:T(8,128)(2,1)} %fusion.70), channel_id=1, source_target_pairs={{0,1},{1,0},{2,3},{3,2},{4,5},{5,4},{6,7},{7,6},{8,9},{9,8},{10,11... | collective-permute-start | bytes 1572872 | tf_op jit(solution)/shard_map/ppermute | solution.py:78
  220.0 56.0 %copy-start.11 = (pred[256,8]{0,1:T(8,128)(4,1)S(1)}, pred[256,8]{0,1:T(8,128)(4,1)}, u32[]{:S(2)}) copy-start(pred[256,8]{0,1:T(8,128)(4,1)} %copy-done.10) | copy-start | bytes 6148
  220.0 56.0 %copy-start.13 = (s32[256,8]{0,1:T(8,128)S(1)}, s32[256,8]{0,1:T(8,128)}, u32[]{:S(2)}) copy-start(s32[256,8]{0,1:T(8,128)} %copy-done.12) | copy-start | bytes 24580
  220.0 19.8 %all-to-all-start.3 = ((bf16[8,64,1024]{2,1,0:T(8,128)(2,1)}), bf16[8,64,1024]{2,1,0:T(8,128)(2,1)}, u32[]{:S(2)}, u32[]{:S(2)}) async-start(bf16[8,64,1024]{2,1,0:T(8,128)(2,1)} %bitcast.178), calls=%async_computation.3 | async-start | bytes 2097152 | tf_op jit(solution)/shard_map/all_to_all | solution.py:134
  228.3 35.1 %collective-permute-start.5 = (bf16[256,1024]{1,0:T(8,128)(2,1)}, bf16[256,1024]{1,0:T(8,128)(2,1)}, u32[]{:S(2)}, u32[]{:S(2)}) collective-permute-start(bf16[256,1024]{1,0:T(8,128)(2,1)} %fusion.71), channel_id=1, source_target_pairs={{0,2},{1,3},{2,0},{3,1},{4,6},{5,7},{6,4},{7,5},{8,10},{9,11},{10,... | collective-permute-start | bytes 1572872 | tf_op jit(solution)/shard_map/ppermute | solution.py:78
  230.9 45.2 %collective-permute-start.8 = (bf16[256,1024]{1,0:T(8,128)(2,1)}, bf16[256,1024]{1,0:T(8,128)(2,1)}, u32[]{:S(2)}, u32[]{:S(2)}) collective-permute-start(bf16[256,1024]{1,0:T(8,128)(2,1)} %fusion.72), channel_id=1, source_target_pairs={{0,3},{1,2},{2,1},{3,0},{4,7},{5,6},{6,5},{7,4},{8,11},{9,10},{10,... | collective-permute-start | bytes 1572872 | tf_op jit(solution)/shard_map/ppermute | solution.py:78
where the time goes:
time: 281 us; the launch traced here: 279 us
  waiting for transfers between devices  110 us (39%)
  matrix products  71.2 us (25%)
  starting transfers between devices  61.2 us (22%)
  other arithmetic  20.7 us (7%)
  local copies, waits for them, and re-layouts  15.5 us (6%)
    ppermute x9, waiting for transfers between devices, swapped(): return lax.ppermute(rows, 'group', [(i, i ^ step) for i in range(groups)])  62 us
    dot_general x4, matrix products, body(): partial = jnp.dot(hidden, expert_out[0], preferred_element_type=jnp.float32)  37.4 us
    all_to_all x4, waiting for transfers between devices, body(): lax.all_to_all(outbox.reshape(shards, capacity, channels), 'tm', split_ax...  23.6 us
    all_to_all x4, starting transfers between devices, body(): lax.all_to_all(partial.astype(jnp.bfloat16).reshape(shards, capacity, cha...  22.7 us
    all_to_all x4, starting transfers between devices, body(): lax.all_to_all(outbox.reshape(shards, capacity, channels), 'tm', split_ax...  21 us
    all_to_all x4, waiting for transfers between devices, body(): lax.all_to_all(partial.astype(jnp.bfloat16).reshape(shards, capacity, cha...  18.8 us
    dot_general x4, matrix products, body(): mixed = jnp.dot(back, returned, preferred_element_type=jnp.float32)  10.5 us
    unnamed x51, local copies, waits for them, and re-layouts  9.39 us
  transfers between devices with their start and end apart: 19, of which 13 were waited for; matrix products, arithmetic and copies ran while one was open for 31% of the time, Pallas kernels for 0%

commit v1 on v0

--- a/solution.py
+++ b/solution.py
@@ -87,13 +87,13 @@
     stream_two = (stream_one.astype(jnp.float32) + attended.astype(jnp.float32)).astype(
         jnp.bfloat16
     )
-    stream = lax.all_to_all(
-        stream_two.reshape(shards, 1, across, channels),
-        "tm",
-        split_axis=0,
-        concat_axis=1,
-        tiled=True,
-    ).reshape(spatial, channels)
+    register_plane = lambda unit, which_dim, ndim_at: jnp.concatenate(
+        lax.all_to_all(jnp.stack(jnp.split(unit, lax.axis_size("tm"), which_dim), 0), "tm", 0, 0),
+        ndim_at,
+    )
+    stream = register_plane(stream_two.reshape(shards, 1, across, channels), 0, 1).reshape(
+        spatial, channels
+    )
     home = jnp.arange(shards, dtype=jnp.int32) * classes + mine
     blocks = [swapped(stream, step) for step in range(groups)]
     partials = []

time: 281 us -> 278 us (0.989)
  waiting for transfers between devices: 110 us -> 126 us
  other arithmetic: 20.7 us -> 7.18 us
  matrix products: 71.2 us -> 64.8 us
  local copies, waits for them, and re-layouts: 15.5 us -> 20.2 us
  starting transfers between devices: 61.2 us -> 57.8 us
    ppermute x9, waiting for transfers between devices: 62 us -> 70.5 us  [swapped(): return lax.ppermute(rows, 'group', [(i, i ^ step) for i in range(groups)])]
    unnamed x51 -> x22, local copies, waits for them, and re-layouts: 9.39 us -> 15.1 us
    all_to_all x4, waiting for transfers between devices: 23.6 us -> 28.2 us  [body(): lax.all_to_all(outbox.reshape(shards, capacity, channels), 'tm', split_ax...]
    convert_element_type x4, other arithmetic: 3.74 us -> 0.89 us  [layer_normed(): return ((values - centre) / jnp.sqrt(spread + 1e-05)).astype(jnp.bfloat16)]
  transfers between devices with their start and end apart: 19 -> 19, of which waited for: 13 -> 13; matrix products, arithmetic and copies ran while one was open for 31% -> 23% of each run, Pallas kernels for 0% -> 0%
where the time goes in v1:
time: 278 us; the launch traced here: 277 us
  waiting for transfers between devices  126 us (45%)
  matrix products  64.8 us (23%)
  starting transfers between devices  57.8 us (21%)
  local copies, waits for them, and re-layouts  20.2 us (7%)
  other arithmetic  7.18 us (3%)
    ppermute x9, waiting for transfers between devices, swapped(): return lax.ppermute(rows, 'group', [(i, i ^ step) for i in range(groups)])  70.5 us
    dot_general x4, matrix products, body(): partial = jnp.dot(hidden, expert_out[0], preferred_element_type=jnp.float32)  37 us
    all_to_all x4, waiting for transfers between devices, body(): lax.all_to_all(outbox.reshape(shards, capacity, channels), 'tm', split_ax...  28.2 us
    all_to_all x4, starting transfers between devices, body(): lax.all_to_all(partial.astype(jnp.bfloat16).reshape(shards, capacity, cha...  20.6 us
    all_to_all x4, waiting for transfers between devices, body(): lax.all_to_all(partial.astype(jnp.bfloat16).reshape(shards, capacity, cha...  20 us
    all_to_all x4, starting transfers between devices, body(): lax.all_to_all(outbox.reshape(shards, capacity, channels), 'tm', split_ax...  19.7 us
    unnamed x22, local copies, waits for them, and re-layouts  15.1 us
    dot_general x4, matrix products, body(): mixed = jnp.dot(back, returned, preferred_element_type=jnp.float32)  9.61 us
  transfers between devices with their start and end apart: 19, of which 13 were waited for; matrix products, arithmetic and copies ran while one was open for 23% of the time, Pallas kernels for 0%

profile of v1, /device:TPU:10, one launch (start us, length us, event | category | flops | bytes accessed | tf_op | source)
XLA Modules:
  0.0 276.5 jit_solution(2444450063446270409)
XLA Ops:
  0.5 2.6 collective-permute-start.3
  3.5 4.3 %all-to-all-start = ((bf16[1,8,32,1024]{3,2,0,1:T(8,128)(2,1)}), bf16[1,8,32,1024]{3,2,0,1:T(8,128)(2,1)S(1)}, u32[]{:S(2)}, u32[]{:S(2)}) async-start(bf16[1,8,32,1024]{3,2,0,1:T(8,128)(2,1)} %bitcast.212), calls=%async_computation | async-start | bytes 1048576 | tf_op jit(solution)/shard_map/all_to_all | solution.py:82
  8.6 8.7 %copy.62 = bf16[1024,3072]{0,1:T(8,128)(2,1)} copy(bf16[1024,3072]{1,0:T(8,128)(2,1)} %param.10) | data formatting | bytes 12582912 | tf_op args[2]
  18.7 5.7 %fusion.118 = f32[8,32,3,16,64]{4,1,3,2,0:T(8,128)S(1)} fusion(bf16[3,16,64,1024,1]{3,2,1,0,4:T(8,128)(2,1)} %bitcast.200, bf16[8,32,1024]{2,1,0:T(8,128)(2,1)S(1)} %get-tuple-element.16, f32[8,32]{1,0:T(8,128)S(1)} %add_sqrt_fusion.3, f32[8,32]{1,0:T(8,128)S(1)} %broadcast_multiply_fusion.1), kind=kOutput, calls=%fused_computation.137 | convolution fusion | flops 1611661312 | bytes 9963520 | tf_op jit(solution)/shard_map/dot_general | solution.py:33
  24.4 1.2 multiply_reduce_fusion.1
  25.8 1.4 divide_convert_fusion.2
  27.2 2.8 %fusion.56 = (f32[32,16,8]{2,1,0:T(8,128)S(1)}, f32[32,16,8,8]{2,3,1,0:T(8,128)S(1)}) fusion(bf16[8,32,16,64]{3,1,2,0:T(8,128)(2,1)S(1)} %get-tuple-element.18, bf16[8,32,16,64]{3,1,2,0:T(8,128)(2,1)S(1)} %get-tuple-element.17), kind=kOutput, calls=%fused_computation.61 | convolution fusion | flops 4255744 | bytes 1196032 | tf_op jit(solution)/shard_map/fshd,gshd->shfg/dot_general | solution.py:40
  30.1 1.5 fusion.69
  31.6 1.2 copy.67
  32.8 1.9 reshape.371
  40.7 4.2 %all-to-all-start.1 = ((bf16[8,1,1,32,1024]{4,3,2,1,0:T(8,128)(2,1)}), bf16[8,1,1,32,1024]{4,3,2,1,0:T(8,128)(2,1)S(1)}, u32[]{:S(2)}, u32[]{:S(2)}) async-start(bf16[8,1,1,32,1024]{4,3,2,1,0:T(8,128)(2,1)} %fusion.145), calls=%async_computation.1 | async-start | bytes 1048576 | tf_op jit(solution)/shard_map/all_to_all | solution.py:91
  45.7 7.4 %all-to-all-done.1 = bf16[8,1,1,32,1024]{4,3,2,1,0:T(8,128)(2,1)S(1)} async-done(((bf16[8,1,1,32,1024]{4,3,2,1,0:T(8,128)(2,1)}), bf16[8,1,1,32,1024]{4,3,2,1,0:T(8,128)(2,1)S(1)}, u32[]{:S(2)}, u32[]{:S(2)}) %all-to-all-start.1) | async-done | bytes 524320 | tf_op jit(solution)/shard_map/all_to_all | solution.py:91
  53.2 1.3 collective-permute-start.1
  54.5 2.1 collective-permute-start.4
  58.1 1.5 convolution_convert_fusion.3
  59.5 5.6 %all-to-all-start.2 = ((bf16[8,64,1024]{2,1,0:T(8,128)(2,1)}), bf16[8,64,1024]{2,1,0:T(8,128)(2,1)}, u32[]{:S(2)}, u32[]{:S(2)}) async-start(bf16[8,64,1024]{2,1,0:T(8,128)(2,1)} %bitcast.201), calls=%async_computation.2 | async-start | bytes 2097152 | tf_op jit(solution)/shard_map/all_to_all | solution.py:123
  65.5 11.1 %collective-permute-done.1 = bf16[256,1024]{1,0:T(8,128)(2,1)S(1)} collective-permute-done((bf16[256,1024]{1,0:T(8,128)(2,1)S(1)}, bf16[256,1024]{1,0:T(8,128)(2,1)S(1)}, u32[]{:S(2)}, u32[]{:S(2)}) %collective-permute-start.1) | collective-permute-done | bytes 524320 | tf_op jit(solution)/shard_map/ppermute | solution.py:78
  77.5 14.0 %collective-permute-done.4 = bf16[256,1024]{1,0:T(8,128)(2,1)S(1)} collective-permute-done((bf16[256,1024]{1,0:T(8,128)(2,1)S(1)}, bf16[256,1024]{1,0:T(8,128)(2,1)S(1)}, u32[]{:S(2)}, u32[]{:S(2)}) %collective-permute-start.4) | collective-permute-done | bytes 524320 | tf_op jit(solution)/shard_map/ppermute | solution.py:78
  92.4 10.4 %collective-permute-done.7 = bf16[256,1024]{1,0:T(8,128)(2,1)S(1)} collective-permute-done((bf16[256,1024]{1,0:T(8,128)(2,1)S(1)}, bf16[256,1024]{1,0:T(8,128)(2,1)S(1)}, u32[]{:S(2)}, u32[]{:S(2)}) %collective-permute-start.7) | collective-permute-done | bytes 524320 | tf_op jit(solution)/shard_map/ppermute | solution.py:78
  103.6 1.4 convolution_convert_fusion.2
  105.0 4.2 %all-to-all-start.4 = ((bf16[8,64,1024]{2,1,0:T(8,128)(2,1)}), bf16[8,64,1024]{2,1,0:T(8,128)(2,1)}, u32[]{:S(2)}, u32[]{:S(2)}) async-start(bf16[8,64,1024]{2,1,0:T(8,128)(2,1)} %bitcast.203), calls=%async_computation.4 | async-start | bytes 2097152 | tf_op jit(solution)/shard_map/all_to_all | solution.py:123
  109.5 1.4 convolution_convert_fusion.1
  111.0 11.3 %all-to-all-done.4 = bf16[8,64,1024]{2,1,0:T(8,128)(2,1)} async-done(((bf16[8,64,1024]{2,1,0:T(8,128)(2,1)}), bf16[8,64,1024]{2,1,0:T(8,128)(2,1)}, u32[]{:S(2)}, u32[]{:S(2)}) %all-to-all-start.4) | async-done | bytes 1048608 | tf_op jit(solution)/shard_map/all_to_all | solution.py:123
  122.3 5.0 %all-to-all-start.6 = ((bf16[8,64,1024]{2,1,0:T(8,128)(2,1)}), bf16[8,64,1024]{2,1,0:T(8,128)(2,1)S(1)}, u32[]{:S(2)}, u32[]{:S(2)}) async-start(bf16[8,64,1024]{2,1,0:T(8,128)(2,1)} %bitcast.202), calls=%async_computation.6 | async-start | bytes 2097152 | tf_op jit(solution)/shard_map/all_to_all | solution.py:123
  127.4 1.4 convolution_convert_fusion
  128.8 12.3 %all-to-all-done.6 = bf16[8,64,1024]{2,1,0:T(8,128)(2,1)S(1)} async-done(((bf16[8,64,1024]{2,1,0:T(8,128)(2,1)}), bf16[8,64,1024]{2,1,0:T(8,128)(2,1)S(1)}, u32[]{:S(2)}, u32[]{:S(2)}) %all-to-all-start.6) | async-done | bytes 1048608 | tf_op jit(solution)/shard_map/all_to_all | solution.py:123
  141.2 5.0 %all-to-all-start.8 = ((bf16[8,64,1024]{2,1,0:T(8,128)(2,1)}), bf16[8,64,1024]{2,1,0:T(8,128)(2,1)S(1)}, u32[]{:S(2)}, u32[]{:S(2)}) async-start(bf16[8,64,1024]{2,1,0:T(8,128)(2,1)} %bitcast.48), calls=%async_computation.8 | async-start | bytes 2097152 | tf_op jit(solution)/shard_map/all_to_all | solution.py:123
  146.2 9.3 %fusion.60 = bf16[512,1024]{1,0:T(8,128)(2,1)} fusion(bf16[1,2048,1024]{2,1,0:T(8,128)(2,1)} %param.15, bf16[512,1024]{1,0:T(8,128)(2,1)} %bitcast.37, bf16[1,1024,2048]{2,1,0:T(8,128)(2,1)} %param.14), kind=kOutput, calls=%fused_computation.71 | convolution fusion | flops 4304928768 | bytes 10485760 | tf_op jit(solution)/shard_map/dot_general | solution.py:133
  155.5 4.6 %all-to-all-done.8 = bf16[8,64,1024]{2,1,0:T(8,128)(2,1)S(1)} async-done(((bf16[8,64,1024]{2,1,0:T(8,128)(2,1)}), bf16[8,64,1024]{2,1,0:T(8,128)(2,1)S(1)}, u32[]{:S(2)}, u32[]{:S(2)}) %all-to-all-start.8) | async-done | bytes 1048608 | tf_op jit(solution)/shard_map/all_to_all | solution.py:123
  160.0 1.0 copy-done.4
  161.1 5.0 %all-to-all-start.5 = ((bf16[8,64,1024]{2,1,0:T(8,128)(2,1)}), bf16[8,64,1024]{2,1,0:T(8,128)(2,1)S(1)}, u32[]{:S(2)}, u32[]{:S(2)}) async-start(bf16[8,64,1024]{2,1,0:T(8,128)(2,1)} %bitcast.209), calls=%async_computation.5 | async-start | bytes 2097152 | tf_op jit(solution)/shard_map/all_to_all | solution.py:134
  166.1 9.0 %fusion.63 = bf16[512,1024]{1,0:T(8,128)(2,1)} fusion(bf16[1,2048,1024]{2,1,0:T(8,128)(2,1)} %param.15, bf16[512,1024]{1,0:T(8,128)(2,1)S(1)} %bitcast.205, bf16[1,1024,2048]{2,1,0:T(8,128)(2,1)} %param.14), kind=kOutput, calls=%fused_computation.72 | convolution fusion | flops 4304928768 | bytes 10485760 | tf_op jit(solution)/shard_map/dot_general | solution.py:133
  175.1 4.9 %all-to-all-done.5 = bf16[8,64,1024]{2,1,0:T(8,128)(2,1)S(1)} async-done(((bf16[8,64,1024]{2,1,0:T(8,128)(2,1)}), bf16[8,64,1024]{2,1,0:T(8,128)(2,1)S(1)}, u32[]{:S(2)}, u32[]{:S(2)}) %all-to-all-start.5) | async-done | bytes 1048608 | tf_op jit(solution)/shard_map/all_to_all | solution.py:134
  180.9 5.0 %all-to-all-start.7 = ((bf16[8,64,1024]{2,1,0:T(8,128)(2,1)}), bf16[8,64,1024]{2,1,0:T(8,128)(2,1)S(1)}, u32[]{:S(2)}, u32[]{:S(2)}) async-start(bf16[8,64,1024]{2,1,0:T(8,128)(2,1)} %bitcast.210), calls=%async_computation.7 | async-start | bytes 2097152 | tf_op jit(solution)/shard_map/all_to_all | solution.py:134
  185.9 9.3 %fusion.66 = bf16[512,1024]{1,0:T(8,128)(2,1)} fusion(bf16[1,2048,1024]{2,1,0:T(8,128)(2,1)} %param.15, bf16[512,1024]{1,0:T(8,128)(2,1)} %bitcast.207, bf16[1,1024,2048]{2,1,0:T(8,128)(2,1)} %param.14), kind=kOutput, calls=%fused_computation.73 | convolution fusion | flops 4304928768 | bytes 10485760 | tf_op jit(solution)/shard_map/dot_general | solution.py:133
  195.2 4.6 %all-to-all-done.7 = bf16[8,64,1024]{2,1,0:T(8,128)(2,1)S(1)} async-done(((bf16[8,64,1024]{2,1,0:T(8,128)(2,1)}), bf16[8,64,1024]{2,1,0:T(8,128)(2,1)S(1)}, u32[]{:S(2)}, u32[]{:S(2)}) %all-to-all-start.7) | async-done | bytes 1048608 | tf_op jit(solution)/shard_map/all_to_all | solution.py:134
  199.8 5.0 %all-to-all-start.9 = ((bf16[8,64,1024]{2,1,0:T(8,128)(2,1)}), bf16[8,64,1024]{2,1,0:T(8,128)(2,1)S(1)}, u32[]{:S(2)}, u32[]{:S(2)}) async-start(bf16[8,64,1024]{2,1,0:T(8,128)(2,1)} %bitcast.208), calls=%async_computation.9 | async-start | bytes 2097152 | tf_op jit(solution)/shard_map/all_to_all | solution.py:134
  204.8 9.4 %fusion.57 = bf16[512,1024]{1,0:T(8,128)(2,1)} fusion(bf16[1,2048,1024]{2,1,0:T(8,128)(2,1)} %param.15, bf16[512,1024]{1,0:T(8,128)(2,1)} %bitcast.29, bf16[1,1024,2048]{2,1,0:T(8,128)(2,1)} %param.14), kind=kOutput, calls=%fused_computation.70 | convolution fusion | flops 4304928768 | bytes 10485760 | tf_op jit(solution)/shard_map/dot_general | solution.py:133
  214.2 2.5 fusion.70
  216.7 2.0 all-to-all-done.9
  218.7 5.6 %all-to-all-start.3 = ((bf16[8,64,1024]{2,1,0:T(8,128)(2,1)}), bf16[8,64,1024]{2,1,0:T(8,128)(2,1)}, u32[]{:S(2)}, u32[]{:S(2)}) async-start(bf16[8,64,1024]{2,1,0:T(8,128)(2,1)} %bitcast.206), calls=%async_computation.3 | async-start | bytes 2097152 | tf_op jit(solution)/shard_map/all_to_all | solution.py:134
  224.3 1.3 fusion.71
  225.7 2.7 fusion.72
  228.3 1.5 collective-permute-start.8
  229.8 8.5 %all-to-all-done.3 = bf16[8,64,1024]{2,1,0:T(8,128)(2,1)} async-done(((bf16[8,64,1024]{2,1,0:T(8,128)(2,1)}), bf16[8,64,1024]{2,1,0:T(8,128)(2,1)}, u32[]{:S(2)}, u32[]{:S(2)}) %all-to-all-start.3) | async-done | bytes 1048608 | tf_op jit(solution)/shard_map/all_to_all | solution.py:134
  238.3 22.5 %collective-permute-done.5 = bf16[256,1024]{1,0:T(8,128)(2,1)} collective-permute-done((bf16[256,1024]{1,0:T(8,128)(2,1)}, bf16[256,1024]{1,0:T(8,128)(2,1)}, u32[]{:S(2)}, u32[]{:S(2)}) %collective-permute-start.5) | collective-permute-done | bytes 524320 | tf_op jit(solution)/shard_map/ppermute | solution.py:78
  260.8 12.6 %collective-permute-done.8 = bf16[256,1024]{1,0:T(8,128)(2,1)} collective-permute-done((bf16[256,1024]{1,0:T(8,128)(2,1)}, bf16[256,1024]{1,0:T(8,128)(2,1)}, u32[]{:S(2)}, u32[]{:S(2)}) %collective-permute-start.8) | collective-permute-done | bytes 524320 | tf_op jit(solution)/shard_map/ppermute | solution.py:78
  273.4 3.1 %fusion.116 = bf16[1,256,1024]{2,1,0:T(8,128)(2,1)} fusion(bf16[256,1024]{1,0:T(8,128)(2,1)} %collective-permute-done.8, bf16[256,1024]{1,0:T(8,128)(2,1)} %collective-permute-done.5, bf16[256,1024]{1,0:T(8,128)(2,1)} %collective-permute-done.2, bf16[8,64,1024]{2,1,0:T(8,128)(2,1)} %all-to-all-done.3, bf16[256,1024]{1,0:T(8,128)(2,1)S(1)} %bitcast.199, ...), kind=kOutput, calls=%fused_computation.135 | convolution fusion | flops 271187968 | bytes 3684352 | tf_op jit(solution)/shard_map/dot_general | solution.py:141
  (91 shorter events, 15.9 us)
Async XLA Ops:
  0.0 34.7 %copy-start = (bf16[1024,1024]{1,0:T(8,128)(2,1)S(1)}, bf16[1024,1024]{1,0:T(8,128)(2,1)}, u32[]{:S(2)}) copy-start(bf16[1024,1024]{1,0:T(8,128)(2,1)} %param.11) | copy-start | bytes 6291460
  0.0 17.4 %collective-permute-start = (s32[256,2]{0,1:T(2,128)}, s32[256,2]{0,1:T(2,128)S(1)}, u32[]{:S(2)}, u32[]{:S(2)}) collective-permute-start(s32[256,2]{0,1:T(2,128)} %bitcast.214), channel_id=1, source_target_pairs={{0,1},{1,0},{2,3},{3,2},{4,5},{5,4},{6,7},{7,6},{8,9},{9,8},{10,11... | collective-permute-start | bytes 6152 | tf_op jit(solution)/shard_map/ppermute | solution.py:78
  0.5 16.9 %collective-permute-start.3 = (s32[256,2]{0,1:T(2,128)}, s32[256,2]{0,1:T(2,128)S(1)}, u32[]{:S(2)}, u32[]{:S(2)}) collective-permute-start(s32[256,2]{0,1:T(2,128)} %bitcast.215), channel_id=1, source_target_pairs={{0,2},{1,3},{2,0},{3,1},{4,6},{5,7},{6,4},{7,5},{8,10},{9,11},{10,... | collective-permute-start | bytes 6152 | tf_op jit(solution)/shard_map/ppermute | solution.py:78
  3.0 14.4 %collective-permute-start.6 = (s32[256,2]{0,1:T(2,128)}, s32[256,2]{0,1:T(2,128)S(1)}, u32[]{:S(2)}, u32[]{:S(2)}) collective-permute-start(s32[256,2]{0,1:T(2,128)} %bitcast.216), channel_id=1, source_target_pairs={{0,3},{1,2},{2,1},{3,0},{4,7},{5,6},{6,5},{7,4},{8,11},{9,10},{10,... | collective-permute-start | bytes 6152 | tf_op jit(solution)/shard_map/ppermute | solution.py:78
  3.5 14.3 %all-to-all-start = ((bf16[1,8,32,1024]{3,2,0,1:T(8,128)(2,1)}), bf16[1,8,32,1024]{3,2,0,1:T(8,128)(2,1)S(1)}, u32[]{:S(2)}, u32[]{:S(2)}) async-start(bf16[1,8,32,1024]{3,2,0,1:T(8,128)(2,1)} %bitcast.212), calls=%async_computation | async-start | bytes 1048576 | tf_op jit(solution)/shard_map/all_to_all | solution.py:82
  8.6 8.8 %copy-start.6 = (s32[1,256,2]{1,2,0:T(2,128)S(1)}, s32[1,256,2]{1,2,0:T(2,128)}, u32[]{:S(2)}) copy-start(s32[1,256,2]{1,2,0:T(2,128)} %param.13) | copy-start | bytes 6148
  37.5 27.6 %copy-start.5 = (bf16[1024,16]{0,1:T(8,128)(2,1)S(1)}, bf16[1024,16]{0,1:T(8,128)(2,1)}, u32[]{:S(2)}) copy-start(bf16[1024,16]{0,1:T(8,128)(2,1)} %param.12) | copy-start | bytes 98308
  40.7 12.5 %all-to-all-start.1 = ((bf16[8,1,1,32,1024]{4,3,2,1,0:T(8,128)(2,1)}), bf16[8,1,1,32,1024]{4,3,2,1,0:T(8,128)(2,1)S(1)}, u32[]{:S(2)}, u32[]{:S(2)}) async-start(bf16[8,1,1,32,1024]{4,3,2,1,0:T(8,128)(2,1)} %fusion.145), calls=%async_computation.1 | async-start | bytes 1048576 | tf_op jit(solution)/shard_map/all_to_all | solution.py:91
  53.2 23.4 %collective-permute-start.1 = (bf16[256,1024]{1,0:T(8,128)(2,1)S(1)}, bf16[256,1024]{1,0:T(8,128)(2,1)S(1)}, u32[]{:S(2)}, u32[]{:S(2)}) collective-permute-start(bf16[256,1024]{1,0:T(8,128)(2,1)S(1)} %bitcast.195), channel_id=1, source_target_pairs={{0,1},{1,0},{2,3},{3,2},{4,5},{5,4},{6,7},{7,6},{8,9},{9,8},{10,11... | collective-permute-start | bytes 1572872 | tf_op jit(solution)/shard_map/ppermute | solution.py:78
  54.5 37.0 %collective-permute-start.4 = (bf16[256,1024]{1,0:T(8,128)(2,1)S(1)}, bf16[256,1024]{1,0:T(8,128)(2,1)S(1)}, u32[]{:S(2)}, u32[]{:S(2)}) collective-permute-start(bf16[256,1024]{1,0:T(8,128)(2,1)S(1)} %bitcast.196), channel_id=1, source_target_pairs={{0,2},{1,3},{2,0},{3,1},{4,6},{5,7},{6,4},{7,5},{8,10},{9,11},{10,... | collective-permute-start | bytes 1572872 | tf_op jit(solution)/shard_map/ppermute | solution.py:78
  56.7 46.2 %collective-permute-start.7 = (bf16[256,1024]{1,0:T(8,128)(2,1)S(1)}, bf16[256,1024]{1,0:T(8,128)(2,1)S(1)}, u32[]{:S(2)}, u32[]{:S(2)}) collective-permute-start(bf16[256,1024]{1,0:T(8,128)(2,1)S(1)} %bitcast.197), channel_id=1, source_target_pairs={{0,3},{1,2},{2,1},{3,0},{4,7},{5,6},{6,5},{7,4},{8,11},{9,10},{10,... | collective-permute-start | bytes 1572872 | tf_op jit(solution)/shard_map/ppermute | solution.py:78
  59.5 45.5 %all-to-all-start.2 = ((bf16[8,64,1024]{2,1,0:T(8,128)(2,1)}), bf16[8,64,1024]{2,1,0:T(8,128)(2,1)}, u32[]{:S(2)}, u32[]{:S(2)}) async-start(bf16[8,64,1024]{2,1,0:T(8,128)(2,1)} %bitcast.201), calls=%async_computation.2 | async-start | bytes 2097152 | tf_op jit(solution)/shard_map/all_to_all | solution.py:123
  105.0 17.3 %all-to-all-start.4 = ((bf16[8,64,1024]{2,1,0:T(8,128)(2,1)}), bf16[8,64,1024]{2,1,0:T(8,128)(2,1)}, u32[]{:S(2)}, u32[]{:S(2)}) async-start(bf16[8,64,1024]{2,1,0:T(8,128)(2,1)} %bitcast.203), calls=%async_computation.4 | async-start | bytes 2097152 | tf_op jit(solution)/shard_map/all_to_all | solution.py:123
  122.3 18.9 %all-to-all-start.6 = ((bf16[8,64,1024]{2,1,0:T(8,128)(2,1)}), bf16[8,64,1024]{2,1,0:T(8,128)(2,1)S(1)}, u32[]{:S(2)}, u32[]{:S(2)}) async-start(bf16[8,64,1024]{2,1,0:T(8,128)(2,1)} %bitcast.202), calls=%async_computation.6 | async-start | bytes 2097152 | tf_op jit(solution)/shard_map/all_to_all | solution.py:123
  141.2 18.9 %all-to-all-start.8 = ((bf16[8,64,1024]{2,1,0:T(8,128)(2,1)}), bf16[8,64,1024]{2,1,0:T(8,128)(2,1)S(1)}, u32[]{:S(2)}, u32[]{:S(2)}) async-start(bf16[8,64,1024]{2,1,0:T(8,128)(2,1)} %bitcast.48), calls=%async_computation.8 | async-start | bytes 2097152 | tf_op jit(solution)/shard_map/all_to_all | solution.py:123
  160.0 1.0 copy-start.4
  161.1 18.9 %all-to-all-start.5 = ((bf16[8,64,1024]{2,1,0:T(8,128)(2,1)}), bf16[8,64,1024]{2,1,0:T(8,128)(2,1)S(1)}, u32[]{:S(2)}, u32[]{:S(2)}) async-start(bf16[8,64,1024]{2,1,0:T(8,128)(2,1)} %bitcast.209), calls=%async_computation.5 | async-start | bytes 2097152 | tf_op jit(solution)/shard_map/all_to_all | solution.py:134
  180.0 1.0 copy-start.3
  180.9 18.9 %all-to-all-start.7 = ((bf16[8,64,1024]{2,1,0:T(8,128)(2,1)}), bf16[8,64,1024]{2,1,0:T(8,128)(2,1)S(1)}, u32[]{:S(2)}, u32[]{:S(2)}) async-start(bf16[8,64,1024]{2,1,0:T(8,128)(2,1)} %bitcast.210), calls=%async_computation.7 | async-start | bytes 2097152 | tf_op jit(solution)/shard_map/all_to_all | solution.py:134
  199.8 18.9 %all-to-all-start.9 = ((bf16[8,64,1024]{2,1,0:T(8,128)(2,1)}), bf16[8,64,1024]{2,1,0:T(8,128)(2,1)S(1)}, u32[]{:S(2)}, u32[]{:S(2)}) async-start(bf16[8,64,1024]{2,1,0:T(8,128)(2,1)} %bitcast.208), calls=%async_computation.9 | async-start | bytes 2097152 | tf_op jit(solution)/shard_map/all_to_all | solution.py:134
  216.7 21.6 %collective-permute-start.2 = (bf16[256,1024]{1,0:T(8,128)(2,1)}, bf16[256,1024]{1,0:T(8,128)(2,1)}, u32[]{:S(2)}, u32[]{:S(2)}) collective-permute-start(bf16[256,1024]{1,0:T(8,128)(2,1)} %fusion.70), channel_id=1, source_target_pairs={{0,1},{1,0},{2,3},{3,2},{4,5},{5,4},{6,7},{7,6},{8,9},{9,8},{10,11... | collective-permute-start | bytes 1572872 | tf_op jit(solution)/shard_map/ppermute | solution.py:78
  218.7 7.0 %copy-start.2 = (bf16[8,64,1024]{2,1,0:T(8,128)(2,1)}, bf16[8,64,1024]{2,1,0:T(8,128)(2,1)S(1)}, u32[]{:S(2)}) copy-start(bf16[8,64,1024]{2,1,0:T(8,128)(2,1)S(1)} %all-to-all-done.9) | copy-start | bytes 3145732
  218.7 19.6 %all-to-all-start.3 = ((bf16[8,64,1024]{2,1,0:T(8,128)(2,1)}), bf16[8,64,1024]{2,1,0:T(8,128)(2,1)}, u32[]{:S(2)}, u32[]{:S(2)}) async-start(bf16[8,64,1024]{2,1,0:T(8,128)(2,1)} %bitcast.206), calls=%async_computation.3 | async-start | bytes 2097152 | tf_op jit(solution)/shard_map/all_to_all | solution.py:134
  225.7 35.1 %collective-permute-start.5 = (bf16[256,1024]{1,0:T(8,128)(2,1)}, bf16[256,1024]{1,0:T(8,128)(2,1)}, u32[]{:S(2)}, u32[]{:S(2)}) collective-permute-start(bf16[256,1024]{1,0:T(8,128)(2,1)} %fusion.71), channel_id=1, source_target_pairs={{0,2},{1,3},{2,0},{3,1},{4,6},{5,7},{6,4},{7,5},{8,10},{9,11},{10,... | collective-permute-start | bytes 1572872 | tf_op jit(solution)/shard_map/ppermute | solution.py:78
  225.7 50.9 %copy-start.1 = (bf16[1024,1024]{1,0:T(8,128)(2,1)S(1)}, bf16[1024,1024]{1,0:T(8,128)(2,1)}, u32[]{:S(2)}) copy-start(bf16[1024,1024]{1,0:T(8,128)(2,1)} %param.11) | copy-start | bytes 6291460
  228.3 45.1 %collective-permute-start.8 = (bf16[256,1024]{1,0:T(8,128)(2,1)}, bf16[256,1024]{1,0:T(8,128)(2,1)}, u32[]{:S(2)}, u32[]{:S(2)}) collective-permute-start(bf16[256,1024]{1,0:T(8,128)(2,1)} %fusion.72), channel_id=1, source_target_pairs={{0,3},{1,2},{2,1},{3,0},{4,7},{5,6},{6,5},{7,4},{8,11},{9,10},{10,... | collective-permute-start | bytes 1572872 | tf_op jit(solution)/shard_map/ppermute | solution.py:78
